TPU v7x, 32 devices: a whole 2x2x4 slice. The times are simulated.
32 devices in a mesh: dp: 16 (over z, x, core), tensor: 2 (over y).
Axes of the slice: x: 2, y: 2, z: 4, core: 2. Of those that a mesh axis runs over, the one named last changes fastest.
Arguments:
- inputs: bfloat16 [3152, 768], P('dp'), may hold values from -6 to 6
- norm1_gain: float32 [768], replicated, may hold values from 0.5 to 1.5
- norm1_bias: float32 [768], replicated, may hold values from -4 to 4
- qkv_weight: bfloat16 [3, 768, 768], P(None, None, 'tensor'), may hold values from -0.21875 to 0.21875
- qv_bias: float32 [2, 768], P(None, 'tensor'), may hold values from -4 to 4
- proj_weight: bfloat16 [768, 768], P('tensor'), may hold values from -2 to 2
- proj_bias: float32 [768], replicated, may hold values from -4 to 4
- norm2_gain: float32 [768], replicated, may hold values from 0.5 to 1.5
- norm2_bias: float32 [768], replicated, may hold values from -4 to 4
- router: bfloat16 [768, 16], replicated, may hold values from -0.21582031 to 0.21582031
- expert_in: bfloat16 [16, 768, 3072], P('dp', None, 'tensor'), may hold values from -0.21875 to 0.21875
- expert_in_bias: float32 [16, 3072], P('dp', 'tensor'), may hold values from -4 to 4
- expert_out: bfloat16 [16, 3072, 768], P('dp', 'tensor'), may hold values from -0.109375 to 0.109375
- expert_out_bias: float32 [16, 768], replicated, may hold values from -4 to 4
- routes: int32 [3152, 2], P('dp'), may hold values from 0 to 15, all different within a row; in each aligned block of 197 rows (0 to 196, 197 to 393, ...) at most 42 rows name the same one
- cotangent: bfloat16 [3152, 768], P('dp'), may hold values from -6 to 6
Outputs:
- output: bfloat16 [3152, 768], P('dp')
- input_grad: float32 [3152, 768], P('dp')
- norm1_gain_grad: float32 [768], replicated
- norm1_bias_grad: float32 [768], replicated
- qkv_grad: float32 [3, 768, 768], P(None, None, 'tensor')
- qv_bias_grad: float32 [2, 768], P(None, 'tensor')
- proj_grad: float32 [768, 768], P('tensor')
- proj_bias_grad: float32 [768], replicated
- norm2_gain_grad: float32 [768], replicated
- norm2_bias_grad: float32 [768], replicated
- router_grad: float32 [768, 16], replicated
- expert_in_grad: float32 [16, 768, 3072], P('dp', None, 'tensor')
- expert_in_bias_grad: float32 [16, 3072], P('dp', 'tensor')
- expert_out_grad: float32 [16, 3072, 768], P('dp', 'tensor')
- expert_out_bias_grad: float32 [16, 768], replicated
Inputs may be any that keep to these rules, and one draw needn't show every extreme that they name: `routes`: each token names two different experts; among the tokens of one aligned block of 197 no expert is named more than 42 times, and in some block one expert is named exactly 42 times.
All inputs are finite; a program needn't handle non-finite values.
Results may differ from a plain program's by a relative error of at most 0.011.
Values may be sent and summed in bfloat16 or wider, within the bound.
No kernel may reach another device: no remote copies, remote signals or barrier semaphores. Data moves between devices by JAX's collectives and lax.ppermute only.
A program may use at most 192 MiB of HBM per device.

v0:
```python
import jax
import jax.numpy as jnp
from jax import lax
from jax.sharding import PartitionSpec as P

HEAD = 64
SEQ = 197
epsilon = 1e-06


def norm_parts(values):
    average = jnp.mean(values, axis=-1, keepdims=True)
    centred = values - average
    inverse = lax.rsqrt(jnp.mean(centred * centred, axis=-1, keepdims=True) + epsilon)
    return (centred * inverse, inverse)


def norm_back(inner_grad, normed, inverse):
    first_mean = jnp.mean(inner_grad, axis=-1, keepdims=True)
    second_mean = jnp.mean(inner_grad * normed, axis=-1, keepdims=True)
    return inverse * (inner_grad - first_mean - normed * second_mean)


def gelu_parts(pre_act):
    normal_cdf = 0.5 * (1.0 + lax.erf(pre_act * 0.7071067811865476))
    density = jnp.exp(-0.5 * pre_act * pre_act) * 0.3989422804014327
    return (pre_act * normal_cdf, normal_cdf + pre_act * density)


def local(
    inputs,
    norm1_gain,
    norm1_bias,
    qkv_weight,
    qv_bias,
    proj_weight,
    proj_bias,
    norm2_gain,
    norm2_bias,
    router,
    expert_in,
    expert_in_bias,
    expert_out,
    expert_out_bias,
    routes,
    cotangent,
):
    tok_count = inputs.shape[0]
    feat_dim = inputs.shape[1]
    head_cols = qkv_weight.shape[2]
    heads_here = head_cols // HEAD
    images = tok_count // SEQ
    experts = router.shape[1]
    sources = lax.axis_size("dp")
    group_size = sources // experts
    capacity = max(2, (10 * tok_count + 3 * experts - 1) // (3 * experts))
    score_scale = HEAD ** (-0.5)
    x_in = inputs.astype(jnp.float32)
    normed1, inverse1 = norm_parts(x_in)
    hidden1 = (normed1 * norm1_gain + norm1_bias).astype(jnp.bfloat16)
    projected = jnp.einsum("td,jde->jte", hidden1, qkv_weight, preferred_element_type=jnp.float32)
    bias_rows = jnp.stack([qv_bias[0], jnp.zeros_like(qv_bias[0]), qv_bias[1]])
    projected = (projected + bias_rows[:, None, :]).astype(jnp.bfloat16)
    heads_view = projected.reshape(3, images, SEQ, heads_here, HEAD)
    queries, key_vals, values_in = (heads_view[0], heads_view[1], heads_view[2])
    scores = (
        jnp.einsum("bqhd,bkhd->bhqk", queries, key_vals, preferred_element_type=jnp.float32)
        * score_scale
    )
    row_max = jnp.max(scores, axis=-1, keepdims=True)
    exp_scores = jnp.exp(scores - row_max)
    row_total = jnp.sum(exp_scores, axis=-1, keepdims=True)
    log_total = row_max + jnp.log(row_total)
    prob_low = (exp_scores / row_total).astype(jnp.bfloat16)
    attended = jnp.einsum(
        "bhqk,bkhd->bqhd", prob_low, values_in, preferred_element_type=jnp.float32
    )
    attended = attended.reshape(tok_count, head_cols).astype(jnp.bfloat16)
    attn_part = jnp.dot(attended, proj_weight, preferred_element_type=jnp.float32)
    middle = x_in + lax.psum(attn_part, "tensor") + proj_bias
    normed2, inverse2 = norm_parts(middle)
    hidden2 = (normed2 * norm2_gain + norm2_bias).astype(jnp.bfloat16)
    logits = jnp.dot(hidden2, router, preferred_element_type=jnp.float32)
    expert_ids = jnp.arange(experts, dtype=jnp.int32)
    pick_mask = (routes[:, :, None] == expert_ids[None, None, :]).astype(jnp.float32)
    chosen = jnp.sum(pick_mask * logits[:, None, :], axis=-1)
    chosen_max = jnp.max(chosen, axis=1, keepdims=True)
    chosen_exp = jnp.exp(chosen - chosen_max)
    gate_vals = chosen_exp / jnp.sum(chosen_exp, axis=1, keepdims=True)
    flat_routes = routes.reshape(-1)
    onehot = (flat_routes[:, None] == expert_ids[None, :]).astype(jnp.int32)
    rank_vals = jnp.sum(onehot * (jnp.cumsum(onehot, axis=0) - 1), axis=1)
    slot_index = flat_routes * capacity + rank_vals
    send_rows = jnp.zeros((experts * capacity, feat_dim), jnp.bfloat16)
    send_rows = send_rows.at[slot_index].set(jnp.repeat(hidden2, 2, axis=0))
    send_all = jnp.repeat(send_rows.reshape(experts, capacity, feat_dim), group_size, axis=0)
    arrived = lax.all_to_all(send_all, "dp", split_axis=0, concat_axis=0, tiled=True)
    arrived_flat = arrived.reshape(-1, feat_dim)
    pre_act = (
        jnp.dot(arrived_flat, expert_in[0], preferred_element_type=jnp.float32) + expert_in_bias[0]
    )
    activ_vals, gelu_slope = gelu_parts(pre_act)
    activ_low = activ_vals.astype(jnp.bfloat16)
    part_out = jnp.dot(activ_low, expert_out[0], preferred_element_type=jnp.float32).reshape(
        sources, capacity, feat_dim
    )
    came_back = lax.all_to_all(part_out, "dp", split_axis=0, concat_axis=0, tiled=True)
    local_rows = jnp.sum(came_back.reshape(experts, group_size, capacity, feat_dim), axis=1)
    full_rows = lax.psum(local_rows, "tensor") + expert_out_bias[:, None, :]
    result_rows = full_rows.astype(jnp.bfloat16)
    picked = (
        result_rows.reshape(-1, feat_dim)[slot_index]
        .reshape(tok_count, 2, feat_dim)
        .astype(jnp.float32)
    )
    output = (middle + jnp.sum(gate_vals[:, :, None] * picked, axis=1)).astype(jnp.bfloat16)
    grad_out = cotangent.astype(jnp.float32)
    gate_grad = jnp.sum(picked * grad_out[:, None, :], axis=-1)
    chosen_grad = gate_vals * (gate_grad - jnp.sum(gate_vals * gate_grad, axis=1, keepdims=True))
    logit_grad = jnp.sum(pick_mask * chosen_grad[:, :, None], axis=1).astype(jnp.bfloat16)
    row_grad = (
        (gate_vals[:, :, None] * grad_out[:, None, :]).astype(jnp.bfloat16).reshape(-1, feat_dim)
    )
    out_bias_grad = jnp.einsum(
        "re,rd->ed", onehot.astype(jnp.bfloat16), row_grad, preferred_element_type=jnp.float32
    )
    send_grad = jnp.zeros((experts * capacity, feat_dim), jnp.bfloat16).at[slot_index].set(row_grad)
    send_grad_all = jnp.repeat(send_grad.reshape(experts, capacity, feat_dim), group_size, axis=0)
    grad_arrived = lax.all_to_all(send_grad_all, "dp", split_axis=0, concat_axis=0, tiled=True)
    grad_arrived = grad_arrived.reshape(-1, feat_dim)
    out_weight_grad = jnp.einsum(
        "rf,rd->fd", activ_low, grad_arrived, preferred_element_type=jnp.float32
    )
    act_grad = (
        jnp.einsum("rd,fd->rf", grad_arrived, expert_out[0], preferred_element_type=jnp.float32)
        * gelu_slope
    )
    in_bias_grad = jnp.sum(act_grad, axis=0)
    act_low = act_grad.astype(jnp.bfloat16)
    in_weight_grad = jnp.einsum(
        "rd,rf->df", arrived_flat, act_low, preferred_element_type=jnp.float32
    )
    row_part = jnp.einsum("rf,df->rd", act_low, expert_in[0], preferred_element_type=jnp.float32)
    row_part = row_part.reshape(sources, capacity, feat_dim)
    home_whole = lax.all_to_all(row_part, "dp", split_axis=0, concat_axis=0, tiled=True)
    home_local = jnp.sum(home_whole.reshape(experts, group_size, capacity, feat_dim), axis=1)
    row_back = lax.psum(home_local, "tensor").astype(jnp.bfloat16)
    row_home = (
        row_back.reshape(-1, feat_dim)[slot_index]
        .reshape(tok_count, 2, feat_dim)
        .astype(jnp.float32)
    )
    hidden2_grad = jnp.sum(row_home, axis=1) + jnp.einsum(
        "te,de->td", logit_grad, router, preferred_element_type=jnp.float32
    )
    router_grad = jnp.einsum("td,te->de", hidden2, logit_grad, preferred_element_type=jnp.float32)
    norm2_gain_grad = jnp.sum(hidden2_grad * normed2, axis=0)
    norm2_bias_grad = jnp.sum(hidden2_grad, axis=0)
    middle_grad = grad_out + norm_back(hidden2_grad * norm2_gain, normed2, inverse2)
    proj_bias_grad = jnp.sum(middle_grad, axis=0)
    middle_low = middle_grad.astype(jnp.bfloat16)
    proj_grad = jnp.einsum("tc,td->cd", attended, middle_low, preferred_element_type=jnp.float32)
    attended_grad = jnp.einsum(
        "td,cd->tc", middle_low, proj_weight, preferred_element_type=jnp.float32
    )
    attended_grad = attended_grad.astype(jnp.bfloat16).reshape(images, SEQ, heads_here, HEAD)
    again_scores = (
        jnp.einsum("bqhd,bkhd->bhqk", queries, key_vals, preferred_element_type=jnp.float32)
        * score_scale
    )
    prob_vals = jnp.exp(again_scores - log_total)
    prob_again = prob_vals.astype(jnp.bfloat16)
    value_grad = jnp.einsum(
        "bhqk,bqhd->bkhd", prob_again, attended_grad, preferred_element_type=jnp.float32
    )
    prob_grad = jnp.einsum(
        "bqhd,bkhd->bhqk", attended_grad, values_in, preferred_element_type=jnp.float32
    )
    score_grad = prob_vals * (prob_grad - jnp.sum(prob_vals * prob_grad, axis=-1, keepdims=True))
    score_low = score_grad.astype(jnp.bfloat16)
    query_grad = (
        jnp.einsum("bhqk,bkhd->bqhd", score_low, key_vals, preferred_element_type=jnp.float32)
        * score_scale
    )
    key_grad = (
        jnp.einsum("bhqk,bqhd->bkhd", score_low, queries, preferred_element_type=jnp.float32)
        * score_scale
    )
    proj_low = (
        jnp.stack([query_grad, key_grad, value_grad])
        .reshape(3, tok_count, head_cols)
        .astype(jnp.bfloat16)
    )
    qv_bias_grad = jnp.stack(
        [
            jnp.sum(proj_low[0].astype(jnp.float32), axis=0),
            jnp.sum(proj_low[2].astype(jnp.float32), axis=0),
        ]
    )
    qkv_grad = jnp.einsum("td,jte->jde", hidden1, proj_low, preferred_element_type=jnp.float32)
    hidden1_part = jnp.einsum(
        "jte,jde->td", proj_low, qkv_weight, preferred_element_type=jnp.float32
    )
    hidden1_grad = lax.psum(hidden1_part, "tensor")
    norm1_gain_grad = jnp.sum(hidden1_grad * normed1, axis=0)
    norm1_bias_grad = jnp.sum(hidden1_grad, axis=0)
    input_grad = middle_grad + norm_back(hidden1_grad * norm1_gain, normed1, inverse1)
    summed = lax.psum(
        (
            qkv_grad,
            qv_bias_grad,
            proj_grad,
            proj_bias_grad,
            norm1_gain_grad,
            norm1_bias_grad,
            norm2_gain_grad,
            norm2_bias_grad,
            router_grad,
            out_bias_grad,
        ),
        "dp",
    )
    return (
        output,
        input_grad,
        summed[4],
        summed[5],
        summed[0],
        summed[1],
        summed[2],
        summed[3],
        summed[6],
        summed[7],
        summed[8],
        in_weight_grad[None],
        in_bias_grad[None],
        out_weight_grad[None],
        summed[9],
    )


def solution(mesh):
    return jax.shard_map(
        local,
        mesh=mesh,
        in_specs=(
            P("dp", None),
            P(),
            P(),
            P(None, None, "tensor"),
            P(None, "tensor"),
            P("tensor", None),
            P(),
            P(),
            P(),
            P(),
            P("dp", None, "tensor"),
            P("dp", "tensor"),
            P("dp", "tensor", None),
            P(),
            P("dp", None),
            P("dp", None),
        ),
        out_specs=(
            P("dp", None),
            P("dp", None),
            P(),
            P(),
            P(None, None, "tensor"),
            P(None, "tensor"),
            P("tensor", None),
            P(),
            P(),
            P(),
            P(),
            P("dp", None, "tensor"),
            P("dp", "tensor"),
            P("dp", "tensor", None),
            P(),
        ),
        check_vma=False,
    )
```

profile of v0, /device:TPU:8, one launch (start us, length us, event | category | flops | bytes accessed | tf_op | source)
XLA Modules:
  0.0 654.0 jit_solution(2582611026457275273)
XLA Ops:
  11.0 2.3 fusion.13
  19.0 29.7 %all-reduce.10.cloned.1.call-done = f32[197,768]{1,0:T(8,128)} async-done(((f32[197,768]{1,0:T(8,128)}), f32[197,768]{1,0:T(8,128)}) %all-reduce.10.cloned.1.call-update) | async-done | bytes 605200 | tf_op jit(solution)/shard_map/psum | solution.py:80
  52.3 2.6 reshape.401
  55.0 3.8 scatter_custom_fusion
  58.7 2.2 reshape_broadcast_in_dim_reshape.6
  60.9 6.1 all-to-all-start
  67.0 2.3 mul.261
  69.3 3.1 mul.262
  74.2 1.4 copy.89
  76.7 4.0 scatter_custom_fusion.1
  80.8 2.2 reshape_broadcast_in_dim_reshape.7
  83.0 11.1 %all-to-all-done = bf16[16,42,768]{2,1,0:T(8,128)(2,1)} async-done(((bf16[16,42,768]{2,1,0:T(8,128)(2,1)}), bf16[16,42,768]{2,1,0:T(8,128)(2,1)}, u32[]{:S(2)}, u32[]{:S(2)}) %all-to-all-start) | async-done | bytes 1032224 | tf_op jit(solution)/shard_map/all_to_all | solution.py:97
  94.0 5.7 all-to-all-start.2
  101.0 2.2 reshape.373
  103.2 5.1 multiply_convert_fusion
  108.3 18.4 %all-to-all-done.2 = bf16[16,42,768]{2,1,0:T(8,128)(2,1)} async-done(((bf16[16,42,768]{2,1,0:T(8,128)(2,1)}), bf16[16,42,768]{2,1,0:T(8,128)(2,1)}, u32[]{:S(2)}, u32[]{:S(2)}) %all-to-all-start.2) | async-done | bytes 1032224 | tf_op jit(solution)/shard_map/all_to_all | solution.py:129
  126.7 2.2 reshape.375
  129.0 6.7 %fusion.59 = (f32[1536]{0:T(1024)}, bf16[672,1536]{1,0:T(8,128)(2,1)}) fusion(f32[672,1536]{1,0:T(8,128)} %get-tuple-element.111, f32[1536]{0:T(1024)} %reduce.13, bf16[672,768]{1,0:T(8,128)(2,1)} %reshape.375, bf16[1,1536,768]{2,1,0:T(8,128)(2,1)} %param.28), kind=kOutput, calls=%fused_computation.127 | convolution fusion | flops 1597831680 | bytes 9596928 | tf_op jit(solution)/shard_map/rd,fd->rf/dot_general | solution.py:135
  135.7 4.0 dot_general.82
  139.7 5.1 fusion.5
  144.8 5.7 all-to-all-start.3
  150.5 4.0 dot_general.79
  154.6 5.8 fusion.7
  160.3 41.7 %all-to-all-done.3 = f32[16,42,768]{2,1,0:T(8,128)S(1)} async-done(((f32[16,42,768]{2,1,0:T(8,128)}), f32[16,42,768]{2,1,0:T(8,128)S(1)}, u32[]{:S(2)}, u32[]{:S(2)}) %all-to-all-start.3) | async-done | bytes 2064416 | tf_op jit(solution)/shard_map/all_to_all | solution.py:145
  202.0 6.4 all-to-all-start.1
  208.5 1.8 convert_element_type.118
  210.9 49.0 %all-to-all-done.1 = f32[16,42,768]{2,1,0:T(8,128)} async-done(((f32[16,42,768]{2,1,0:T(8,128)}), f32[16,42,768]{2,1,0:T(8,128)}, u32[]{:S(2)}, u32[]{:S(2)}) %all-to-all-start.1) | async-done | bytes 2064416 | tf_op jit(solution)/shard_map/all_to_all | solution.py:107
  260.1 97.1 %all-reduce.19 = bf16[16,42,768]{2,1,0:T(8,128)(2,1)} all-reduce(f32[16,42,768]{2,1,0:T(8,128)S(1)} %all-to-all-done.3), channel_id=1, replica_groups=mesh['dp'=16,'tensor'=2] {'tensor'}, use_global_device_ids=true, to_apply=%region_17.18 | all-reduce | flops 516096 | bytes 3096576 | tf_op jit(solution)/shard_map/psum | solution.py:147
  358.5 2.2 gather_fusion.1
  361.5 2.4 reduce_sum.254
  363.9 2.5 all-reduce.12.cloned.1.call-done
  366.4 1.9 add_convert_fusion
  368.6 2.7 gather_fusion
  371.3 2.0 reshape.379
  373.3 3.5 multiply_reduce_fusion.1
  377.0 2.3 multiply_reduce_fusion.3
  379.3 1.6 fusion.56
  383.8 3.1 convolution_bitcast_fusion.3
  388.4 2.6 convolution_bitcast_fusion.2
  393.8 6.3 convolution_bitcast_fusion.1
  400.1 4.2 convolution_bitcast_fusion
  406.1 12.9 %all-reduce.14.cloned.1.call-done = f32[197,768]{1,0:T(8,128)} async-done(((f32[197,768]{1,0:T(8,128)}), f32[197,768]{1,0:T(8,128)}) %all-reduce.14.cloned.1.call-update) | async-done | bytes 605200 | tf_op jit(solution)/shard_map/psum | solution.py:204
  419.0 2.1 fusion.30
  421.1 2.1 fusion.29
  423.2 117.6 %all-reduce.18.cloned.1.call-done = (f32[3,768,384]{1,2,0:T(8,128)}, f32[384,768]{1,0:T(8,128)}) async-done(((f32[3,768,384]{1,2,0:T(8,128)}, f32[384,768]{1,0:T(8,128)}), (f32[3,768,384]{1,2,0:T(8,128)}, f32[384,768]{1,0:T(8,128)})) %all-reduce.18.cloned.1.call-update) | async-done | bytes 4718608 | tf_op jit(solution)/shard_map/psum | solution.py:208
  540.8 5.3 copy.104
  546.1 92.2 %all-reduce.16.cloned.1.call-done = (f32[768]{0:T(1024)}, f32[768]{0:T(1024)}, f32[2,384]{1,0:T(2,128)}, f32[768]{0:T(1024)}, f32[768]{0:T(1024)}, /*index=5*/f3...) async-done(((f32[768]{0:T(1024)}, f32[768]{0:T(1024)}, f32[2,384]{1,0:T(2,128)}, f32[768]{0:T(1024)}, f32[768]{0:T(1024)}, /*index=5*/f32[768]{0:T(1024)}, f32[768,16]{0,1:T(8,128)}, ...) | async-done | bytes 116752 | tf_op jit(solution)/shard_map/psum | solution.py:208
  642.1 2.4 copy.131
  (181 shorter events, 36.2 us)
Async XLA Ops:
  7.2 96.0 %copy-start = (bf16[1,768,1536]{2,1,0:T(8,128)(2,1)S(1)}, bf16[1,768,1536]{2,1,0:T(8,128)(2,1)}, u32[]{:S(2)}) copy-start(bf16[1,768,1536]{2,1,0:T(8,128)(2,1)} %param.26) | copy-start | bytes 7077892
  7.2 41.6 %all-reduce.10.cloned.1.call-start = ((), (), s32[]{:S(2)}) async-start(), calls=%async_computation.4 | async-start | bytes 1228800 | tf_op jit(solution)/shard_map/psum | solution.py:80
  13.5 1.4 copy-start.18
  14.2 1.0 copy-start.2
  14.5 1.2 copy-start.11
  14.5 2.4 copy-start.28
  15.2 3.8 copy-start.20
  15.2 33.6 %copy-start.5 = (bf16[197,768]{1,0:T(8,128)(2,1)S(1)}, bf16[197,768]{1,0:T(8,128)(2,1)}, u32[]{:S(2)}) copy-start(bf16[197,768]{1,0:T(8,128)(2,1)} %param.16) | copy-start | bytes 907780
  15.2 33.6 %copy-start.39 = (f32[768]{0:T(1024)S(1)}, f32[768]{0:T(1024)}, u32[]{:S(2)}) copy-start(f32[768]{0:T(1024)} %param.22) | copy-start | bytes 9220
  16.9 33.4 %copy-start.26 = (f32[768]{0:T(1024)S(1)}, f32[768]{0:T(1024)}, u32[]{:S(2)}) copy-start(f32[768]{0:T(1024)} %param.23) | copy-start | bytes 9220
  16.9 33.4 %copy-start.40 = (f32[768]{0:T(1024)S(1)}, f32[768]{0:T(1024)}, u32[]{:S(2)}) copy-start(f32[768]{0:T(1024)} %param.24) | copy-start | bytes 9220
  50.3 10.7 %copy-start.32 = (f32[197]{0:T(256)}, f32[197]{0:T(256)S(1)}, u32[]{:S(2)}) copy-start(f32[197]{0:T(256)S(1)} %add_rsqrt_fusion) | copy-start | bytes 2368
  60.9 33.1 %all-to-all-start = ((bf16[16,42,768]{2,1,0:T(8,128)(2,1)}), bf16[16,42,768]{2,1,0:T(8,128)(2,1)}, u32[]{:S(2)}, u32[]{:S(2)}) async-start(bf16[16,42,768]{2,1,0:T(8,128)(2,1)} %reshape_broadcast_in_dim_reshape.6), calls=%async_computation | async-start | bytes 2359296 | tf_op jit(solution)/shard_map/all_to_all | solution.py:97
  67.0 5.4 copy-start.22
  76.7 6.2 copy-start.29
  94.0 32.7 %all-to-all-start.2 = ((bf16[16,42,768]{2,1,0:T(8,128)(2,1)}), bf16[16,42,768]{2,1,0:T(8,128)(2,1)}, u32[]{:S(2)}, u32[]{:S(2)}) async-start(bf16[16,42,768]{2,1,0:T(8,128)(2,1)} %reshape_broadcast_in_dim_reshape.7), calls=%async_computation.2 | async-start | bytes 2359296 | tf_op jit(solution)/shard_map/all_to_all | solution.py:129
  144.8 57.2 %all-to-all-start.3 = ((f32[16,42,768]{2,1,0:T(8,128)}), f32[16,42,768]{2,1,0:T(8,128)S(1)}, u32[]{:S(2)}, u32[]{:S(2)}) async-start(f32[16,42,768]{2,1,0:T(8,128)} %fusion.5), calls=%async_computation.3 | async-start | bytes 4718592 | tf_op jit(solution)/shard_map/all_to_all | solution.py:145
  202.0 57.9 %all-to-all-start.1 = ((f32[16,42,768]{2,1,0:T(8,128)}), f32[16,42,768]{2,1,0:T(8,128)}, u32[]{:S(2)}, u32[]{:S(2)}) async-start(f32[16,42,768]{2,1,0:T(8,128)} %fusion.7), calls=%async_computation.1 | async-start | bytes 4718592 | tf_op jit(solution)/shard_map/all_to_all | solution.py:107
  208.5 157.9 %all-reduce.12.cloned.1.call-start = ((), (), s32[]{:S(2)}) async-start(), calls=%async_computation.5 | async-start | bytes 4718592 | tf_op jit(solution)/shard_map/psum | solution.py:109
  260.0 98.5 %copy-start.31 = (s32[1024]{0:T(1024)S(1)}, s32[1024]{0:T(1024)}, u32[]{:S(2)}) copy-start(s32[1024]{0:T(1024)} %pad_clamp_fusion) | copy-start | bytes 12292
  260.0 159.0 %all-reduce.14.cloned.1.call-start = ((), (), s32[]{:S(2)}) async-start(), calls=%async_computation.6 | async-start | bytes 1228800 | tf_op jit(solution)/shard_map/psum | solution.py:204
  360.7 5.7 copy-start.23
  368.6 4.7 copy-start.17
  371.2 2.0 copy-start.9
  371.2 5.6 copy-start.35
  371.3 5.7 copy-start.33
  373.3 6.0 copy-start.8
  376.9 2.4 copy-start.10
  377.0 3.9 copy-start.12
  379.2 2.2 copy-start.3
  383.7 3.3 copy-start.21
  386.9 1.4 copy-start.27
  386.9 1.4 copy-start.37
  386.9 1.4 copy-start.44
  387.0 153.8 %all-reduce.18.cloned.1.call-start = ((), (), s32[]{:S(2)}) async-start(), calls=%async_computation.8 | async-start | bytes 9437184 | tf_op jit(solution)/shard_map/psum | solution.py:208
  391.0 1.3 copy-start.4
  391.0 1.3 copy-start.30
  391.0 2.2 copy-start.38
  391.0 247.2 %all-reduce.16.cloned.1.call-start = ((), (), s32[]{:S(2)}) async-start(), calls=%async_computation.7 | async-start | bytes 243712 | tf_op jit(solution)/shard_map/psum | solution.py:208
  393.8 6.3 copy-start.13
  393.8 6.3 copy-start.16
  400.1 5.2 copy-start.7
  540.8 106.7 %copy-start.1 = (bf16[1,768,1536]{2,1,0:T(8,128)(2,1)S(1)}, bf16[1,768,1536]{2,1,0:T(8,128)(2,1)}, u32[]{:S(2)}) copy-start(bf16[1,768,1536]{2,1,0:T(8,128)(2,1)} %param.26) | copy-start | bytes 7077892
  638.3 6.2 copy-start.43
  638.3 6.8 %copy-start.42 = (f32[768]{0:T(1024)S(1)}, f32[768]{0:T(1024)}, u32[]{:S(2)}) copy-start(f32[768]{0:T(1024)} %get-tuple-element.125) | copy-start | bytes 9220
  638.3 7.4 %copy-start.41 = (f32[768]{0:T(1024)S(1)}, f32[768]{0:T(1024)}, u32[]{:S(2)}) copy-start(f32[768]{0:T(1024)} %get-tuple-element.126) | copy-start | bytes 9220
  638.3 8.0 %copy-start.25 = (f32[768,16]{0,1:T(8,128)S(1)}, f32[768,16]{0,1:T(8,128)}, u32[]{:S(2)}) copy-start(f32[768,16]{0,1:T(8,128)} %get-tuple-element.127) | copy-start | bytes 147460
  638.3 8.6 %copy-start.24 = (f32[16,768]{1,0:T(8,128)S(1)}, f32[16,768]{1,0:T(8,128)}, u32[]{:S(2)}) copy-start(f32[16,768]{1,0:T(8,128)} %get-tuple-element.131) | copy-start | bytes 147460
  (6 other events, 4.4 us)
Sparse Core Ops, SparseCore 0:
  17.0 31.7 all-reduce.9
  260.1 106.2 all-reduce.11
  387.1 31.8 all-reduce.13
  423.5 117.2 all-reduce.17
  546.8 91.3 all-reduce.15
where the time goes:
time: 656 us; the launch traced here: 654 us
  waiting for transfers between devices  375 us (57%)
  blocking collectives  97.1 us (15%)
  local copies, waits for them, and re-layouts  63 us (10%)
  matrix products  51.2 us (8%)
  other arithmetic  28.9 us (4%)
  starting transfers between devices  24.3 us (4%)
  between operations  14.3 us (2%)
    psum x2, waiting for transfers between devices, local(): lax.psum((qkv_grad, qv_bias_grad, proj_grad, proj_bias_grad, norm1_gain_g...  210 us
    psum x1, blocking collectives, local(): row_back = lax.psum(home_local, 'tensor').astype(jnp.bfloat16)  97.1 us
    all_to_all x1, waiting for transfers between devices, local(): lax.all_to_all(part_out, 'dp', split_axis=0, concat_axis=0, tiled=True)  49 us
    all_to_all x1, waiting for transfers between devices, local(): lax.all_to_all(row_part, 'dp', split_axis=0, concat_axis=0, tiled=True)  41.7 us
    psum x1, waiting for transfers between devices, local(): middle = x_in + lax.psum(attn_part, 'tensor') + proj_bias  29.7 us
    all_to_all x1, waiting for transfers between devices, local(): lax.all_to_all(send_grad_all, 'dp', split_axis=0, concat_axis=0, tiled=True)  18.4 us
    unnamed x101, local copies, waits for them, and re-layouts  18.2 us
  transfers between devices with their start and end apart: 9, of which 9 were waited for; matrix products, arithmetic and copies ran while one was open for 11% of the time, Pallas kernels for 0%

commit v1 on v0

--- a/solution.py
+++ b/solution.py
@@ -6,6 +6,11 @@
 HEAD = 64
 SEQ = 197
 epsilon = 1e-06
+
+
+def stages_all_pair(content):
+    passed = jnp.sum(lax.all_gather(content, "tensor"), 0)
+    return passed
 
 
 def norm_parts(values):
@@ -144,7 +149,7 @@
     row_part = row_part.reshape(sources, capacity, feat_dim)
     home_whole = lax.all_to_all(row_part, "dp", split_axis=0, concat_axis=0, tiled=True)
     home_local = jnp.sum(home_whole.reshape(experts, group_size, capacity, feat_dim), axis=1)
-    row_back = lax.psum(home_local, "tensor").astype(jnp.bfloat16)
+    row_back = stages_all_pair(home_local).astype(jnp.bfloat16)
     row_home = (
         row_back.reshape(-1, feat_dim)[slot_index]
         .reshape(tok_count, 2, feat_dim)

time: 656 us -> 614 us (0.936); the launches traced: 654 us -> 604 us
  blocking collectives: 97.1 us -> 0 us
  waiting for transfers between devices: 375 us -> 419 us
    psum x1 -> x0, blocking collectives: 97.1 us -> none  [local(): row_back = lax.psum(home_local, 'tensor').astype(jnp.bfloat16)]
    all_gather x0 -> x1, waiting for transfers between devices: none -> 47.7 us  [stages_all_pair(): passed = jnp.sum(lax.all_gather(content, 'tensor'), 0)]
    all_to_all x1, waiting for transfers between devices: 49 us -> 33.5 us  [local(): lax.all_to_all(part_out, 'dp', split_axis=0, concat_axis=0, tiled=True)]
    psum x1, waiting for transfers between devices: 2.51 us -> 16.1 us  [local(): full_rows = lax.psum(local_rows, 'tensor') + expert_out_bias[:, None, :]]
    all_to_all x1, waiting for transfers between devices: 18.4 us -> 8.41 us  [local(): lax.all_to_all(send_grad_all, 'dp', split_axis=0, concat_axis=0, tiled=True)]
    all_to_all x1, waiting for transfers between devices: 41.7 us -> 50.7 us  [local(): lax.all_to_all(row_part, 'dp', split_axis=0, concat_axis=0, tiled=True)]
    unnamed x101 -> x97, local copies, waits for them, and re-layouts: 18.2 us -> 19 us
  transfers between devices with their start and end apart: 9 -> 10, of which waited for: 9 -> 10; matrix products, arithmetic and copies ran while one was open for 11% -> 16% of each run, Pallas kernels for 0% -> 0%
where the time goes in v1:
time: 614 us; the launch traced here: 604 us
  waiting for transfers between devices  419 us (68%)
  local copies, waits for them, and re-layouts  65.6 us (11%)
  matrix products  50 us (8%)
  other arithmetic  29 us (5%)
  starting transfers between devices  25.2 us (4%)
  between operations  14.9 us (2%)
    psum x2, waiting for transfers between devices, local(): lax.psum((qkv_grad, qv_bias_grad, proj_grad, proj_bias_grad, norm1_gain_g...  210 us
    all_to_all x1, waiting for transfers between devices, local(): lax.all_to_all(row_part, 'dp', split_axis=0, concat_axis=0, tiled=True)  50.7 us
    all_gather x1, waiting for transfers between devices, stages_all_pair(): passed = jnp.sum(lax.all_gather(content, 'tensor'), 0)  47.7 us
    all_to_all x1, waiting for transfers between devices, local(): lax.all_to_all(part_out, 'dp', split_axis=0, concat_axis=0, tiled=True)  33.5 us
    psum x1, waiting for transfers between devices, local(): middle = x_in + lax.psum(attn_part, 'tensor') + proj_bias  29.7 us
    unnamed x97, local copies, waits for them, and re-layouts  19 us
    psum x1, waiting for transfers between devices, local(): full_rows = lax.psum(local_rows, 'tensor') + expert_out_bias[:, None, :]  16.1 us
  transfers between devices with their start and end apart: 10, of which 10 were waited for; matrix products, arithmetic and copies ran while one was open for 16% of the time, Pallas kernels for 0%

profile of v1, /device:TPU:8, one launch (start us, length us, event | category | flops | bytes accessed | tf_op | source)
XLA Modules:
  0.0 603.9 jit_solution(4496185938288408508)
XLA Ops:
  11.0 2.3 fusion.13
  19.0 29.7 %all-reduce.9.cloned.1.call-done = f32[197,768]{1,0:T(8,128)} async-done(((f32[197,768]{1,0:T(8,128)}), f32[197,768]{1,0:T(8,128)}) %all-reduce.9.cloned.1.call-update) | async-done | bytes 605200 | tf_op jit(solution)/shard_map/psum | solution.py:85
  52.3 2.6 reshape.401
  55.0 3.8 scatter_custom_fusion
  58.7 2.2 reshape_broadcast_in_dim_reshape.6
  60.9 6.1 %all-to-all-start = ((bf16[16,42,768]{2,1,0:T(8,128)(2,1)}), bf16[16,42,768]{2,1,0:T(8,128)(2,1)}, u32[]{:S(2)}, u32[]{:S(2)}) async-start(bf16[16,42,768]{2,1,0:T(8,128)(2,1)} %reshape_broadcast_in_dim_reshape.6), calls=%async_computation | async-start | bytes 2359296 | tf_op jit(solution)/shard_map/all_to_all | solution.py:102
  67.0 2.3 mul.261
  69.3 3.1 mul.262
  74.2 1.4 copy.130
  76.7 4.0 scatter_custom_fusion.1
  80.7 2.2 reshape_broadcast_in_dim_reshape.7
  83.0 11.0 %all-to-all-done = bf16[16,42,768]{2,1,0:T(8,128)(2,1)} async-done(((bf16[16,42,768]{2,1,0:T(8,128)(2,1)}), bf16[16,42,768]{2,1,0:T(8,128)(2,1)}, u32[]{:S(2)}, u32[]{:S(2)}) %all-to-all-start) | async-done | bytes 1032224 | tf_op jit(solution)/shard_map/all_to_all | solution.py:102
  94.0 6.3 %all-to-all-start.2 = ((bf16[16,42,768]{2,1,0:T(8,128)(2,1)}), bf16[16,42,768]{2,1,0:T(8,128)(2,1)}, u32[]{:S(2)}, u32[]{:S(2)}) async-start(bf16[16,42,768]{2,1,0:T(8,128)(2,1)} %reshape_broadcast_in_dim_reshape.7), calls=%async_computation.2 | async-start | bytes 2359296 | tf_op jit(solution)/shard_map/all_to_all | solution.py:134
  101.6 2.2 reshape.374
  103.9 5.1 multiply_convert_fusion
  109.0 4.0 dot_general.79
  113.0 5.8 fusion.7
  118.8 8.4 %all-to-all-done.2 = bf16[16,42,768]{2,1,0:T(8,128)(2,1)} async-done(((bf16[16,42,768]{2,1,0:T(8,128)(2,1)}), bf16[16,42,768]{2,1,0:T(8,128)(2,1)}, u32[]{:S(2)}, u32[]{:S(2)}) %all-to-all-start.2) | async-done | bytes 1032224 | tf_op jit(solution)/shard_map/all_to_all | solution.py:134
  127.2 5.7 all-to-all-start.1
  132.9 2.2 reshape.376
  135.1 6.7 %fusion.59 = (f32[1536]{0:T(1024)}, bf16[672,1536]{1,0:T(8,128)(2,1)}) fusion(f32[672,1536]{1,0:T(8,128)} %get-tuple-element.141, f32[1536]{0:T(1024)} %reduce.13, bf16[672,768]{1,0:T(8,128)(2,1)} %reshape.376, bf16[1,1536,768]{2,1,0:T(8,128)(2,1)} %param.28), kind=kOutput, calls=%fused_computation.127 | convolution fusion | flops 1597831680 | bytes 9596928 | tf_op jit(solution)/shard_map/rd,fd->rf/dot_general | solution.py:140
  141.8 4.0 dot_general.82
  145.8 5.1 fusion.5
  150.9 33.5 %all-to-all-done.1 = f32[16,42,768]{2,1,0:T(8,128)} async-done(((f32[16,42,768]{2,1,0:T(8,128)}), f32[16,42,768]{2,1,0:T(8,128)}, u32[]{:S(2)}, u32[]{:S(2)}) %all-to-all-start.1) | async-done | bytes 2064416 | tf_op jit(solution)/shard_map/all_to_all | solution.py:112
  184.4 6.6 %all-to-all-start.3 = ((f32[16,42,768]{2,1,0:T(8,128)}), f32[16,42,768]{2,1,0:T(8,128)S(1)}, u32[]{:S(2)}, u32[]{:S(2)}) async-start(f32[16,42,768]{2,1,0:T(8,128)} %fusion.5), calls=%async_computation.3 | async-start | bytes 4718592 | tf_op jit(solution)/shard_map/all_to_all | solution.py:150
  191.7 50.7 %all-to-all-done.3 = f32[16,42,768]{2,1,0:T(8,128)S(1)} async-done(((f32[16,42,768]{2,1,0:T(8,128)}), f32[16,42,768]{2,1,0:T(8,128)S(1)}, u32[]{:S(2)}, u32[]{:S(2)}) %all-to-all-start.3) | async-done | bytes 2064416 | tf_op jit(solution)/shard_map/all_to_all | solution.py:150
  242.4 2.5 copy.136
  246.8 16.1 %all-reduce.11.cloned.1.call-done = f32[16,42,768]{2,1,0:T(8,128)} async-done(((f32[16,42,768]{2,1,0:T(8,128)}), f32[16,42,768]{2,1,0:T(8,128)}) %all-reduce.11.cloned.1.call-update) | async-done | bytes 2064400 | tf_op jit(solution)/shard_map/psum | solution.py:114
  262.9 1.9 add_convert_fusion
  265.1 2.7 gather_fusion
  267.7 2.0 reshape.379
  269.7 3.5 multiply_reduce_fusion.1
  273.4 47.7 %all-gather.3.cloned.1.call-done = f32[32,42,768]{2,0,1:T(8,128)} async-done(((f32[16,42,768]{2,0,1:T(8,128)}), f32[32,42,768]{2,0,1:T(8,128)}) %all-gather.3.cloned.1.call-update) | async-done | bytes 4128784 | tf_op jit(solution)/shard_map/all_gather | solution.py:12
  321.1 2.6 reduce_sum.263
  324.4 2.2 gather_fusion.1
  327.4 1.4 reduce_sum.264
  329.9 1.6 fusion.56
  334.5 3.1 convolution_bitcast_fusion.3
  339.0 2.6 convolution_bitcast_fusion.2
  344.4 6.3 %convolution_bitcast_fusion.1 = f32[1,768,1536]{2,1,0:T(8,128)} fusion(bf16[672,768]{1,0:T(8,128)(2,1)} %reshape.374, bf16[672,1536]{1,0:T(8,128)(2,1)} %get-tuple-element.130), kind=kOutput, calls=%fused_computation.13 | convolution fusion | flops 1585446912 | bytes 7815168 | tf_op jit(solution)/shard_map/rd,rf->df/dot_general | solution.py:145
  350.7 4.2 convolution_bitcast_fusion
  356.7 11.6 %all-reduce.13.cloned.1.call-done = f32[197,768]{1,0:T(8,128)} async-done(((f32[197,768]{1,0:T(8,128)}), f32[197,768]{1,0:T(8,128)}) %all-reduce.13.cloned.1.call-update) | async-done | bytes 605200 | tf_op jit(solution)/shard_map/psum | solution.py:209
  368.3 2.1 fusion.30
  370.4 2.1 fusion.29
  372.6 117.6 %all-reduce.17.cloned.1.call-done = (f32[3,768,384]{1,2,0:T(8,128)}, f32[384,768]{1,0:T(8,128)}) async-done(((f32[3,768,384]{1,2,0:T(8,128)}, f32[384,768]{1,0:T(8,128)}), (f32[3,768,384]{1,2,0:T(8,128)}, f32[384,768]{1,0:T(8,128)})) %all-reduce.17.cloned.1.call-update) | async-done | bytes 4718608 | tf_op jit(solution)/shard_map/psum | solution.py:213
  490.2 5.3 copy.147
  495.5 92.1 %all-reduce.15.cloned.1.call-done = (f32[768]{0:T(1024)}, f32[768]{0:T(1024)}, f32[2,384]{1,0:T(2,128)}, f32[768]{0:T(1024)}, f32[768]{0:T(1024)}, /*index=5*/f3...) async-done(((f32[768]{0:T(1024)}, f32[768]{0:T(1024)}, f32[2,384]{1,0:T(2,128)}, f32[768]{0:T(1024)}, f32[768]{0:T(1024)}, /*index=5*/f32[768]{0:T(1024)}, f32[768,16]{0,1:T(8,128)}, ...) | async-done | bytes 116752 | tf_op jit(solution)/shard_map/psum | solution.py:213
  591.4 2.4 copy.172
  (182 shorter events, 38.3 us)
Async XLA Ops:
  7.2 96.7 %copy-start = (bf16[1,768,1536]{2,1,0:T(8,128)(2,1)S(1)}, bf16[1,768,1536]{2,1,0:T(8,128)(2,1)}, u32[]{:S(2)}) copy-start(bf16[1,768,1536]{2,1,0:T(8,128)(2,1)} %param.26) | copy-start | bytes 7077892
  7.2 41.6 %all-reduce.9.cloned.1.call-start = ((), (), s32[]{:S(2)}) async-start(), calls=%async_computation.4 | async-start | bytes 1228800 | tf_op jit(solution)/shard_map/psum | solution.py:85
  13.5 1.4 copy-start.19
  14.2 1.0 copy-start.2
  14.5 1.2 copy-start.12
  14.5 2.4 copy-start.29
  15.2 3.8 copy-start.21
  15.2 33.5 %copy-start.5 = (bf16[197,768]{1,0:T(8,128)(2,1)S(1)}, bf16[197,768]{1,0:T(8,128)(2,1)}, u32[]{:S(2)}) copy-start(bf16[197,768]{1,0:T(8,128)(2,1)} %param.16) | copy-start | bytes 907780
  15.2 33.5 %copy-start.37 = (f32[768]{0:T(1024)S(1)}, f32[768]{0:T(1024)}, u32[]{:S(2)}) copy-start(f32[768]{0:T(1024)} %param.22) | copy-start | bytes 9220
  16.9 33.4 %copy-start.27 = (f32[768]{0:T(1024)S(1)}, f32[768]{0:T(1024)}, u32[]{:S(2)}) copy-start(f32[768]{0:T(1024)} %param.23) | copy-start | bytes 9220
  16.9 33.4 %copy-start.38 = (f32[768]{0:T(1024)S(1)}, f32[768]{0:T(1024)}, u32[]{:S(2)}) copy-start(f32[768]{0:T(1024)} %param.24) | copy-start | bytes 9220
  19.0 35.9 %copy-start.34 = (s32[394,1]{0,1:T(1,128)}, s32[394,1]{0,1:T(1,128)S(1)}, u32[]{:S(2)}) copy-start(s32[394,1]{0,1:T(1,128)S(1)} %compare_select_fusion) | copy-start | bytes 4732
  60.9 33.1 %all-to-all-start = ((bf16[16,42,768]{2,1,0:T(8,128)(2,1)}), bf16[16,42,768]{2,1,0:T(8,128)(2,1)}, u32[]{:S(2)}, u32[]{:S(2)}) async-start(bf16[16,42,768]{2,1,0:T(8,128)(2,1)} %reshape_broadcast_in_dim_reshape.6), calls=%async_computation | async-start | bytes 2359296 | tf_op jit(solution)/shard_map/all_to_all | solution.py:102
  67.0 5.4 copy-start.23
  94.0 33.2 %all-to-all-start.2 = ((bf16[16,42,768]{2,1,0:T(8,128)(2,1)}), bf16[16,42,768]{2,1,0:T(8,128)(2,1)}, u32[]{:S(2)}, u32[]{:S(2)}) async-start(bf16[16,42,768]{2,1,0:T(8,128)(2,1)} %reshape_broadcast_in_dim_reshape.7), calls=%async_computation.2 | async-start | bytes 2359296 | tf_op jit(solution)/shard_map/all_to_all | solution.py:134
  127.2 57.2 %all-to-all-start.1 = ((f32[16,42,768]{2,1,0:T(8,128)}), f32[16,42,768]{2,1,0:T(8,128)}, u32[]{:S(2)}, u32[]{:S(2)}) async-start(f32[16,42,768]{2,1,0:T(8,128)} %fusion.7), calls=%async_computation.1 | async-start | bytes 4718592 | tf_op jit(solution)/shard_map/all_to_all | solution.py:112
  184.4 58.1 %all-to-all-start.3 = ((f32[16,42,768]{2,1,0:T(8,128)}), f32[16,42,768]{2,1,0:T(8,128)S(1)}, u32[]{:S(2)}, u32[]{:S(2)}) async-start(f32[16,42,768]{2,1,0:T(8,128)} %fusion.5), calls=%async_computation.3 | async-start | bytes 4718592 | tf_op jit(solution)/shard_map/all_to_all | solution.py:150
  190.9 71.9 %all-reduce.11.cloned.1.call-start = ((), (), s32[]{:S(2)}) async-start(), calls=%async_computation.5 | async-start | bytes 4718592 | tf_op jit(solution)/shard_map/psum | solution.py:114
  191.7 129.4 %all-gather.3.cloned.1.call-start = ((), (), s32[]{:S(2)}) async-start(), calls=%async_computation.7 | async-start | bytes 6193152 | tf_op jit(solution)/shard_map/all_gather | solution.py:12
  244.9 1.0 copy-start.8
  244.9 1.8 copy-start.35
  244.9 17.9 %copy-start.24 = (f32[16,768]{1,0:T(8,128)S(1)}, f32[16,768]{1,0:T(8,128)}, u32[]{:S(2)}) copy-start(f32[16,768]{1,0:T(8,128)} %param.29) | copy-start | bytes 147460
  245.0 123.3 %all-reduce.13.cloned.1.call-start = ((), (), s32[]{:S(2)}) async-start(), calls=%async_computation.6 | async-start | bytes 1228800 | tf_op jit(solution)/shard_map/psum | solution.py:209
  265.1 4.7 copy-start.18
  267.7 2.0 copy-start.10
  267.7 5.6 copy-start.31
  327.4 2.5 copy-start.9
  328.8 1.1 copy-start.11
  328.8 2.7 copy-start.13
  329.9 2.1 copy-start.3
  332.8 0.9 copy-start.16
  334.3 3.3 copy-start.22
  337.6 1.4 copy-start.28
  337.6 1.4 copy-start.33
  337.6 1.4 copy-start.42
  337.6 152.6 %all-reduce.17.cloned.1.call-start = ((), (), s32[]{:S(2)}) async-start(), calls=%async_computation.9 | async-start | bytes 9437184 | tf_op jit(solution)/shard_map/psum | solution.py:213
  341.6 1.3 copy-start.4
  341.6 2.2 copy-start.36
  341.7 245.9 %all-reduce.15.cloned.1.call-start = ((), (), s32[]{:S(2)}) async-start(), calls=%async_computation.8 | async-start | bytes 243712 | tf_op jit(solution)/shard_map/psum | solution.py:213
  344.4 6.3 %copy-start.14 = (bf16[672,1536]{1,0:T(8,128)(2,1)S(1)}, bf16[672,1536]{1,0:T(8,128)(2,1)}, u32[]{:S(2)}) copy-start(bf16[672,1536]{1,0:T(8,128)(2,1)} %get-tuple-element.140) | copy-start | bytes 6193156
  344.4 6.3 %copy-start.17 = (bf16[672,768]{1,0:T(8,128)(2,1)S(1)}, bf16[672,768]{1,0:T(8,128)(2,1)}, u32[]{:S(2)}) copy-start(bf16[672,768]{1,0:T(8,128)(2,1)} %reshape.376) | copy-start | bytes 3096580
  350.7 4.2 copy-start.7
  490.2 106.7 %copy-start.1 = (bf16[1,768,1536]{2,1,0:T(8,128)(2,1)S(1)}, bf16[1,768,1536]{2,1,0:T(8,128)(2,1)}, u32[]{:S(2)}) copy-start(bf16[1,768,1536]{2,1,0:T(8,128)(2,1)} %param.26) | copy-start | bytes 7077892
  587.6 6.2 %copy-start.41 = (f32[768]{0:T(1024)S(1)}, f32[768]{0:T(1024)}, u32[]{:S(2)}) copy-start(f32[768]{0:T(1024)} %get-tuple-element.154) | copy-start | bytes 9220
  587.6 6.8 %copy-start.40 = (f32[768]{0:T(1024)S(1)}, f32[768]{0:T(1024)}, u32[]{:S(2)}) copy-start(f32[768]{0:T(1024)} %get-tuple-element.155) | copy-start | bytes 9220
  587.6 7.4 %copy-start.39 = (f32[768]{0:T(1024)S(1)}, f32[768]{0:T(1024)}, u32[]{:S(2)}) copy-start(f32[768]{0:T(1024)} %get-tuple-element.156) | copy-start | bytes 9220
  587.6 8.0 %copy-start.26 = (f32[768,16]{0,1:T(8,128)S(1)}, f32[768,16]{0,1:T(8,128)}, u32[]{:S(2)}) copy-start(f32[768,16]{0,1:T(8,128)} %get-tuple-element.157) | copy-start | bytes 147460
  587.6 8.6 %copy-start.25 = (f32[16,768]{1,0:T(8,128)S(1)}, f32[16,768]{1,0:T(8,128)}, u32[]{:S(2)}) copy-start(f32[16,768]{1,0:T(8,128)} %get-tuple-element.161) | copy-start | bytes 147460
  (5 other events, 3.5 us)
Sparse Core Ops, SparseCore 0:
  17.0 31.7 all-reduce.8
  194.1 68.7 all-reduce.10
  265.1 56.0 all-gather.2
  337.7 30.5 all-reduce.12
  372.9 117.2 all-reduce.16
  496.2 91.3 all-reduce.14
